TPU v7x, 512 devices: a whole 4x4x16 slice. The times are simulated.
512 devices in a mesh: ep: 32 (over z_lo, x), blk: 16 (over y, z_hi, core).
Axes of the slice: x: 4, y: 4, z: 16 (z_hi: 2, z_lo: 8; z = z_hi * 8 + z_lo), core: 2. Of those that a mesh axis runs over, the one named last changes fastest.
Arguments:
- tokens: bfloat16 [65536, 1536], P(('ep', 'blk')), may hold values from -6 to 6
- norm_gain: bfloat16 [1536], replicated, may hold values from 0.099609375 to 1.8984375
- router_weight: bfloat16 [1536, 32], replicated, may hold values from -0.15625 to 0.15625
- routes: int32 [65536, 4], P(('ep', 'blk')), may hold values from 0 to 31, all different within a row; in each aligned block of 128 rows (0 to 127, 128 to 255, ...) at most 24 rows name the same one
- placement: int32 [32], replicated, may hold values from 0 to 31, each once
- gate_weight: bfloat16 [32, 1536, 768], P('ep', 'blk'), may hold values from -0.15625 to 0.15625
- up_weight: bfloat16 [32, 1536, 768], P('ep', 'blk'), may hold values from -0.15625 to 0.15625
- down_weight: bfloat16 [32, 768, 1536], P('ep', 'blk'), may hold values from -0.21875 to 0.21875
Outputs:
- mixed: bfloat16 [65536, 1536], P(('ep', 'blk'))
Inputs may be any that keep to these rules, and one draw needn't show every extreme that they name: `routes`: among the rows of one device, each expert is named by at most 24 rows, a bound that some block reaches; a row names 4 different experts. `placement`: each index of ep holds exactly one expert.
All inputs are finite; a program needn't handle non-finite values.
Results may differ from a plain program's by a relative error of at most 0.0071.
Values may be sent and summed in bfloat16 or wider, within the bound.
A program may use at most 64 MiB of HBM per device.

v0:
```python
import jax
import jax.numpy as jnp
from jax import lax
from jax.sharding import PartitionSpec as P


def add_product(left, piece):
    return jnp.dot(left, piece, preferred_element_type=jnp.float32)


def on_device(
    tokens, norm_gain, router_weight, routes, placement, gate_weight, up_weight, down_weight
):
    tok_rows = tokens.shape[0]
    width = tokens.shape[1]
    top_count = routes.shape[1]
    experts = router_weight.shape[1]
    holders = lax.axis_size("ep")
    capacity = 3 * tok_rows * top_count // (2 * experts)
    values = tokens.astype(jnp.float32)
    square = jnp.mean(values * values, axis=-1, keepdims=True)
    normed = (values * lax.rsqrt(square + 1e-06) * norm_gain.astype(jnp.float32)).astype(
        jnp.bfloat16
    )
    logits = jnp.dot(normed, router_weight, preferred_element_type=jnp.float32)
    picked = jax.nn.sigmoid(jnp.take_along_axis(logits, routes, axis=1))
    gates = picked / jnp.sum(picked, axis=1, keepdims=True)
    flat_ids = routes.reshape(-1)
    onehot = flat_ids[:, None] == jnp.arange(experts, dtype=jnp.int32)[None, :]
    counts = jnp.cumsum(onehot.astype(jnp.int32), axis=0)
    slots = jnp.sum(jnp.where(onehot, counts - 1, 0), axis=1)
    target = jnp.sum(jnp.where(onehot, placement[None, :], 0), axis=1)
    repeated = jnp.repeat(normed, top_count, axis=0)
    outgoing = jnp.zeros((holders, capacity, width), jnp.bfloat16).at[target, slots].set(repeated)
    incoming = lax.all_to_all(outgoing, "ep", split_axis=0, concat_axis=0, tiled=True)
    expert_in = incoming.reshape(holders * capacity, width)

    def add_gate(piece):
        return add_product(expert_in, piece)

    gate = add_gate(lax.all_gather(gate_weight[0], "blk", axis=0, tiled=True))
    upper = add_gate(lax.all_gather(up_weight[0], "blk", axis=0, tiled=True))
    hidden = (jax.nn.relu(gate) * upper).astype(jnp.bfloat16)
    summed_out = add_product(hidden, lax.all_gather(down_weight[0], "blk", axis=0, tiled=True))
    expert_out = summed_out.astype(jnp.bfloat16)
    returned = lax.all_to_all(
        expert_out.reshape(holders, capacity, width), "ep", split_axis=0, concat_axis=0, tiled=True
    )
    collected = returned[target, slots].astype(jnp.float32)
    summed = jnp.sum(collected.reshape(tok_rows, top_count, width) * gates[:, :, None], axis=1)
    return summed.astype(jnp.bfloat16)


def solution(mesh):
    in_specs = (
        P(("ep", "blk"), None),
        P(),
        P(),
        P(("ep", "blk"), None),
        P(),
        P("ep", "blk", None),
        P("ep", "blk", None),
        P("ep", "blk", None),
    )
    out_specs = P(("ep", "blk"), None)
    return jax.shard_map(
        on_device, mesh=mesh, in_specs=in_specs, out_specs=out_specs, check_vma=False
    )
```

profile of v0, /device:TPU:1, one launch (start us, length us, event | category | flops | bytes accessed | tf_op | source)
XLA Modules:
  0.0 481.4 jit_solution(1658468891097099509)
XLA Ops:
  6.5 0.7 all-gather.9.cloned.1.call-update
  7.3 0.8 copy.18
  8.3 1.2 reduce-window.6
  9.7 0.7 convert_element_type.32
  10.4 1.2 fusion.7
  11.6 1.2 fusion.9
  12.8 0.7 copy-done.1
  13.5 0.4 broadcast_in_dim.37
  13.9 0.4 reshape.112
  14.4 1.6 broadcast_in_dim.22
  16.1 79.8 %scatter_fusion = bf16[32,24,1536]{2,1,0:T(8,128)(2,1)} fusion(bf16[32,24,1536]{2,1,0:T(8,128)(2,1)} %broadcast_in_dim.22, s32[512]{0:T(512)S(1)} %bitcast.43, bf16[512,1536]{1,0:T(8,128)(2,1)S(1)} %reshape.112), kind=kCustom, calls=%fused_computation.2 | custom fusion | bytes 4722688 | tf_op jit(solution)/shard_map/scatter | solution.py:34
  95.9 16.0 %all-to-all-start = ((bf16[32,24,1536]{2,1,0:T(8,128)(2,1)}), bf16[32,24,1536]{2,1,0:T(8,128)(2,1)S(1)}, u32[]{:S(2)}, u32[]{:S(2)}) async-start(bf16[32,24,1536]{2,1,0:T(8,128)(2,1)} %scatter_fusion), calls=%async_computation | async-start | bytes 4718592 | tf_op jit(solution)/shard_map/all_to_all | solution.py:35
  112.0 0.7 all-gather.11.cloned.1.call-update
  112.7 0.7 all-gather.7.cloned.1.call-update
  113.4 136.1 %all-to-all-done = bf16[32,24,1536]{2,1,0:T(8,128)(2,1)S(1)} async-done(((bf16[32,24,1536]{2,1,0:T(8,128)(2,1)}), bf16[32,24,1536]{2,1,0:T(8,128)(2,1)S(1)}, u32[]{:S(2)}, u32[]{:S(2)}) %all-to-all-start) | async-done | bytes 2359328 | tf_op jit(solution)/shard_map/all_to_all | solution.py:35
  249.6 5.1 %fusion.1 = f32[768,768]{1,0:T(8,128)} fusion(bf16[768,1536]{1,0:T(8,128)(2,1)S(1)} %bitcast.44, bf16[1,1536,768]{2,1,0:T(8,128)(2,1)} %all-gather.9.cloned.1.call-done), kind=kOutput, calls=%fused_computation.6 | convolution fusion | flops 1811939328 | bytes 7077888 | tf_op jit(solution)/shard_map/dot_general | solution.py:8
  254.7 83.8 %all-gather.7.cloned.1.call-done = bf16[1,1536,768]{2,1,0:T(8,128)(2,1)} async-done(((bf16[1,96,768]{2,1,0:T(8,128)(2,1)}), bf16[1,1536,768]{2,1,0:T(8,128)(2,1)}) %all-gather.7.cloned.1.call-update) | async-done | bytes 2359312 | tf_op jit(solution)/shard_map/all_gather | solution.py:41
  338.5 9.1 %convolution_convert_fusion = bf16[768,1536]{1,0:T(8,128)(2,1)} fusion(bf16[1,768,1536]{2,1,0:T(8,128)(2,1)} %all-gather.11.cloned.1.call-done, f32[768,768]{1,0:T(8,128)} %fusion.1, bf16[768,1536]{1,0:T(8,128)(2,1)S(1)} %bitcast.45, bf16[1,1536,768]{2,1,0:T(8,128)(2,1)} %all-gather.7.cloned.1.call-done), kind=kOutput, calls=%fused_computation.3 | convolution fusion | flops 3626827776 | bytes 11796480 | tf_op jit(solution)/shard_map/dot_general | solution.py:8
  347.6 5.0 %all-to-all-start.1 = ((bf16[32,24,1536]{2,1,0:T(8,128)(2,1)}), bf16[32,24,1536]{2,1,0:T(8,128)(2,1)S(1)}, u32[]{:S(2)}, u32[]{:S(2)}) async-start(bf16[32,24,1536]{2,1,0:T(8,128)(2,1)} %bitcast.46), calls=%async_computation.1 | async-start | bytes 4718592 | tf_op jit(solution)/shard_map/all_to_all | solution.py:46
  353.0 3.8 gather_fusion.1
  357.2 102.1 %all-to-all-done.1 = bf16[32,24,1536]{2,1,0:T(8,128)(2,1)S(1)} async-done(((bf16[32,24,1536]{2,1,0:T(8,128)(2,1)}), bf16[32,24,1536]{2,1,0:T(8,128)(2,1)S(1)}, u32[]{:S(2)}, u32[]{:S(2)}) %all-to-all-start.1) | async-done | bytes 2359328 | tf_op jit(solution)/shard_map/all_to_all | solution.py:46
  459.3 9.7 %gather_fusion = bf16[512,1536]{1,0:T(8,128)(2,1)} fusion(bf16[32,24,1536]{2,1,0:T(8,128)(2,1)S(1)} %all-to-all-done.1, s32[512]{0:T(512)S(1)} %bitcast.42), kind=kCustom, calls=%fused_computation | custom fusion | bytes 3149824 | tf_op jit(solution)/shard_map/gather | solution.py:49
  468.9 2.9 reshape.97
  471.8 3.0 multiply_reduce_fusion
  (32 shorter events, 1.5 us)
Async XLA Ops:
  6.5 346.3 %copy-start = (bf16[1536,32]{0,1:T(8,128)(2,1)S(1)}, bf16[1536,32]{0,1:T(8,128)(2,1)}, u32[]{:S(2)}) copy-start(bf16[1536,32]{0,1:T(8,128)(2,1)} %param.10) | copy-start | bytes 294916
  6.5 106.9 %all-gather.9.cloned.1.call-start = ((), (), s32[]{:S(2)}) async-start(), calls=%async_computation.3 | async-start | bytes 2506752 | tf_op jit(solution)/shard_map/all_gather | solution.py:42
  12.7 0.7 copy-start.1
  13.5 0.8 copy-start.4
  95.9 153.7 %all-to-all-start = ((bf16[32,24,1536]{2,1,0:T(8,128)(2,1)}), bf16[32,24,1536]{2,1,0:T(8,128)(2,1)S(1)}, u32[]{:S(2)}, u32[]{:S(2)}) async-start(bf16[32,24,1536]{2,1,0:T(8,128)(2,1)} %scatter_fusion), calls=%async_computation | async-start | bytes 4718592 | tf_op jit(solution)/shard_map/all_to_all | solution.py:35
  111.9 142.8 %all-gather.11.cloned.1.call-start = ((), (), s32[]{:S(2)}) async-start(), calls=%async_computation.4 | async-start | bytes 2506752 | tf_op jit(solution)/shard_map/all_gather | solution.py:44
  112.7 225.8 %all-gather.7.cloned.1.call-start = ((), (), s32[]{:S(2)}) async-start(), calls=%async_computation.2 | async-start | bytes 2506752 | tf_op jit(solution)/shard_map/all_gather | solution.py:41
  347.6 5.0 %copy-start.3 = (s32[128,4]{0,1:T(4,128)S(1)}, s32[128,4]{0,1:T(4,128)}, u32[]{:S(2)}) copy-start(s32[128,4]{0,1:T(4,128)} %param.11) | copy-start | bytes 6148
  347.6 5.3 %copy-start.2 = (bf16[128,1536]{1,0:T(8,128)(2,1)S(1)}, bf16[128,1536]{1,0:T(8,128)(2,1)}, u32[]{:S(2)}) copy-start(bf16[128,1536]{1,0:T(8,128)(2,1)} %copy-done.1) | copy-start | bytes 1179652
  347.6 111.7 %all-to-all-start.1 = ((bf16[32,24,1536]{2,1,0:T(8,128)(2,1)}), bf16[32,24,1536]{2,1,0:T(8,128)(2,1)S(1)}, u32[]{:S(2)}, u32[]{:S(2)}) async-start(bf16[32,24,1536]{2,1,0:T(8,128)(2,1)} %bitcast.46), calls=%async_computation.1 | async-start | bytes 4718592 | tf_op jit(solution)/shard_map/all_to_all | solution.py:46
Sparse Core Ops, SparseCore 0:
  10.6 101.6 all-gather.8
  116.0 104.8 all-gather.10
  224.3 114.1 all-gather.6
where the time goes:
time: 484 us; the launch traced here: 481 us
  waiting for transfers between devices  324 us (67%)
  local copies, waits for them, and re-layouts  101 us (21%)
  starting transfers between devices  21.1 us (4%)
  matrix products  14.4 us (3%)
  between operations  13.3 us (3%)
  other arithmetic  7.45 us (2%)
    all_to_all x1, waiting for transfers between devices, on_device(): lax.all_to_all(outgoing, 'ep', split_axis=0, concat_axis=0, tiled=True)  136 us
    all_to_all x1, waiting for transfers between devices, on_device(): lax.all_to_all(expert_out.reshape(holders, capacity, width), 'ep', split_...  102 us
    all_gather x1, waiting for transfers between devices, on_device(): gate = add_gate(lax.all_gather(gate_weight[0], 'blk', axis=0, tiled=True))  83.8 us
    scatter x1, local copies, waits for them, and re-layouts, on_device(): jnp.zeros((holders, capacity, width), jnp.bfloat16).at[target, slots]  79.8 us
    all_to_all x1, starting transfers between devices, on_device(): lax.all_to_all(outgoing, 'ep', split_axis=0, concat_axis=0, tiled=True)  16 us
    dot_general x2, matrix products, add_product(): return jnp.dot(left, piece, preferred_element_type=jnp.float32)  14.2 us
    gather x1, local copies, waits for them, and re-layouts, on_device(): collected = returned[target, slots].astype(jnp.float32)  9.69 us
  transfers between devices with their start and end apart: 5, of which 3 were waited for; matrix products, arithmetic and copies ran while one was open for 20% of the time, Pallas kernels for 0%

commit v1 on v0

v1 whole, which is shorter than its diff:
```python
import functools

import jax
import jax.numpy as jnp
from jax import lax
from jax.experimental import pallas as pl
from jax.experimental.pallas import tpu as pltpu
from jax.sharding import PartitionSpec as P

MESH = pl.DeviceIdType.MESH
NZ, NX, NY = 8, 4, 4
CAP = 24
LAG_EXPERT = 4
LAG_MIX = 5
LAG_SUM = 6
STEPS = NZ - 1 + LAG_SUM
WEIGHTS_AT = 5
AG_PIECES = 2
RS_PIECES = 4


def kernel(
    tokens, gain, routes_t, router_t, placement, gate_w, up_w, down_w, out,
    tok, met, wgu, wdn, rel_gu, rel_dn, xs, xr, ys, yr, hid, part, rin_b, rin_f, rout,
    loc_sem, z_s, z_r, yo_s, yo_r, yp_s, yp_r, y2_s, y2_r, c_s, c_r,
    ag_s, ag_r, mg_s, mg_r, xd_s, xd_r, xb_s, xb_r, rs_s, rs_rb, rs_rf,
):
    f32, bf16 = jnp.float32, jnp.bfloat16
    ep, blk = lax.axis_index("ep"), lax.axis_index("blk")
    z, x = ep // NX, ep % NX
    y, zh, c = blk // 4, (blk // 2) % 2, blk % 2
    width = tokens.shape[1]
    rows = tokens.shape[0]
    grows, drows = gate_w.shape[0], down_w.shape[0]
    ff = gate_w.shape[1]

    def blk_of(yy, zz, cc):
        return ((yy + NY) % NY) * 4 + zz * 2 + cc

    def at_z(zz):
        return {"ep": zz * NX + x, "blk": blk}

    def at_x(xx):
        return {"ep": z * NX + xx, "blk": blk}

    up4 = {"ep": ((z + 4) % NZ) * NX + x, "blk": blk_of(y, (zh + z // 4) % 2, c)}
    dn4_zh = (zh + 1 - z // 4) % 2
    dn4 = {"ep": ((z + 4) % NZ) * NX + x, "blk": blk_of(y, dn4_zh, c)}
    up4_zh = (zh + z // 4) % 2
    y_up = {"ep": ep, "blk": blk_of(y + 1, zh, c)}
    y_dn = {"ep": ep, "blk": blk_of(y - 1, zh, c)}
    core = {"ep": ep, "blk": blk_of(y, zh, 1 - c)}

    def remote(src, dst, s, r, dev):
        return pltpu.make_async_remote_copy(
            src_ref=src, dst_ref=dst, send_sem=s, recv_sem=r, device_id=dev, device_id_type=MESH
        )

    def gu_at(b):
        return wgu.at[pl.ds(pl.multiple_of(b * grows, grows), grows)]

    def dn_at(b):
        return wdn.at[pl.ds(pl.multiple_of(b * drows, drows), drows)]

    own = pl.ds(pl.multiple_of(blk * grows, grows), grows)
    local = [
        pltpu.make_async_copy(gate_w, wgu.at[own, pl.ds(0, ff)], loc_sem.at[0]),
        pltpu.make_async_copy(up_w, wgu.at[own, pl.ds(ff, ff)], loc_sem.at[1]),
        pltpu.make_async_copy(down_w, dn_at(blk), loc_sem.at[2]),
    ]
    for copy in local:
        copy.start()

    barrier = pltpu.get_barrier_semaphore()

    def greet(dev):
        pl.semaphore_signal(barrier, inc=1, device_id=dev, device_id_type=MESH)

    for dev in (up4, dn4, y_up, y_dn, core):
        greet(dev)
    for j in range(1, NX):
        greet(at_x((x + j) % NX))

    @pl.when(z > 0)
    def _():
        greet(at_z(z - 1))

    @pl.when(z < NZ - 1)
    def _():
        greet(at_z(z + 1))

    peers = 8 + (z > 0).astype(jnp.int32) + (z < NZ - 1).astype(jnp.int32)
    pl.semaphore_wait(barrier, peers)

    for copy in local:
        copy.wait()

    half_g, half_d = grows // 2, width // 2

    def gu_half(b, h):
        return wgu.at[pl.ds(pl.multiple_of(b * grows + h * half_g, half_g), half_g)]

    def dn_half(b, h):
        return wdn.at[pl.ds(pl.multiple_of(b * drows, drows), drows), pl.ds(h * half_d, half_d)]

    hop1, hop2 = [], []
    for h, dev, owner in ((0, up4, blk_of(y, dn4_zh, c)), (1, dn4, blk_of(y, up4_zh, c))):
        hop1 += [
            remote(gu_half(blk, h), rel_gu.at[h], z_s.at[0, h, 0], z_r.at[0, h, 0], dev),
            remote(dn_half(blk, h), rel_dn.at[h], z_s.at[0, h, 1], z_r.at[0, h, 1], dev),
        ]
        hop2 += [
            remote(rel_gu.at[h], gu_half(owner, h), z_s.at[1, h, 0], z_r.at[1, h, 0], dev),
            remote(rel_dn.at[h], dn_half(owner, h), z_s.at[1, h, 1], z_r.at[1, h, 1], dev),
        ]
    mate = blk_of(y, 1 - zh, c)

    def shard_to(b, s, r, dev):
        return [
            remote(gu_at(b), gu_at(b), s.at[0], r.at[0], dev),
            remote(dn_at(b), dn_at(b), s.at[1], r.at[1], dev),
        ]

    def start(copies):
        for copy in copies:
            copy.start()

    def wait_recv(copies):
        for copy in copies:
            copy.wait_recv()

    def wait_send(copies):
        for copy in copies:
            copy.wait_send()

    mine_up = shard_to(blk, yo_s.at[0], yo_r.at[0], y_up)
    mine_dn = shard_to(blk, yo_s.at[1], yo_r.at[1], y_dn)
    from_dn = shard_to(blk_of(y - 1, zh, c), yo_s.at[0], yo_r.at[0], y_dn)
    from_up = shard_to(blk_of(y + 1, zh, c), yo_s.at[1], yo_r.at[1], y_up)
    mate_up = shard_to(mate, yp_s.at[0], yp_r.at[0], y_up)
    mate_dn = shard_to(mate, yp_s.at[1], yp_r.at[1], y_dn)
    mate_from_dn = shard_to(blk_of(y - 1, 1 - zh, c), yp_s.at[0], yp_r.at[0], y_dn)
    mate_from_up = shard_to(blk_of(y + 1, 1 - zh, c), yp_s.at[1], yp_r.at[1], y_up)
    far_own = shard_to(blk_of(y - 1, zh, c), y2_s.at[0], y2_r.at[0], y_up)
    far_mate = shard_to(blk_of(y + 1, 1 - zh, c), y2_s.at[1], y2_r.at[1], y_dn)
    far_own_in = shard_to(blk_of(y - 2, zh, c), y2_s.at[0], y2_r.at[0], y_dn)
    far_mate_in = shard_to(blk_of(y + 2, 1 - zh, c), y2_s.at[1], y2_r.at[1], y_up)
    held = [(0, zh), (-1, zh), (1, zh), (2, zh), (0, 1 - zh), (-1, 1 - zh), (1, 1 - zh), (2, 1 - zh)]
    to_core = [shard_to(blk_of(y + dy, zz, c), c_s.at[k], c_r.at[k], core) for k, (dy, zz) in enumerate(held)]
    of_core = [shard_to(blk_of(y + dy, zz, 1 - c), c_s.at[k], c_r.at[k], core) for k, (dy, zz) in enumerate(held)]

    start(hop1)
    start(mine_up)
    start(mine_dn)
    start(to_core[0])

    values = tokens[...].astype(f32)
    square = jnp.mean(values * values, axis=-1, keepdims=True)
    normed = (values * lax.rsqrt(square + 1e-06) * gain[...].astype(f32)).astype(bf16)
    tok[z] = normed
    experts = router_t.shape[0]
    holder = lax.broadcasted_iota(jnp.int32, (experts, experts), 0)
    placed = (holder == placement[...]).astype(f32).astype(bf16)
    expert_row = lax.broadcasted_iota(jnp.int32, (experts, rows), 0)
    named = jnp.zeros((experts, rows), f32)
    for k in range(routes_t.shape[0]):
        named = named + (expert_row == routes_t[pl.ds(k, 1), :]).astype(f32)
    named = jnp.dot(placed, named.astype(bf16), preferred_element_type=f32)
    earlier = lax.broadcasted_iota(jnp.int32, (rows, rows), 0) < lax.broadcasted_iota(
        jnp.int32, (rows, rows), 1
    )
    before = jnp.dot(named.astype(bf16), earlier.astype(f32).astype(bf16), preferred_element_type=f32)
    slot = jnp.where(named > 0.5, before + 1.0, 0.0)
    router_p = jnp.dot(placed, router_t[...], preferred_element_type=f32).astype(bf16)
    logits = lax.dot_general(
        router_p, normed, (((1,), (1,)), ((), ())), preferred_element_type=f32
    )
    picked = jnp.where(named > 0.5, jax.nn.sigmoid(logits), 0.0)
    gates = picked / jnp.sum(picked, axis=0, keepdims=True)
    for zz in range(NZ):
        met[z, zz, pl.ds(0, NX), :] = slot[zz * NX : (zz + 1) * NX]
        met[z, zz, pl.ds(NX, NX), :] = gates[zz * NX : (zz + 1) * NX]

    piece = rows // AG_PIECES

    def block_to(way, s, d, zz):
        copies = [remote(met.at[s], met.at[s], mg_s.at[way, d], mg_r.at[way, d], at_z(zz))]
        for p in range(AG_PIECES):
            part_of = tok.at[s, pl.ds(p * piece, piece)]
            copies.append(remote(part_of, part_of, ag_s.at[way, d, p], ag_r.at[way, d, p], at_z(zz)))
        return copies

    @pl.when(z < NZ - 1)
    def _():
        start(block_to(0, z, 1, z + 1))

    @pl.when(z > 0)
    def _():
        start(block_to(1, z, 1, z - 1))

    for one, two in zip(hop1, hop2):
        one.wait_recv()
        two.start()
    wait_recv(from_dn)
    start(far_own)
    start(to_core[1])
    wait_recv(from_up)
    start(to_core[2])

    def pair_at(d):
        left = (z + d) % 2 == 0
        q = jnp.where(left, (z - d) // 2, (z + d - 1) // 2)
        valid = jnp.logical_and(d >= 1, jnp.where(left, z - d >= 0, z + d - 1 <= NZ - 1))
        return jnp.where(valid, q, 0), valid

    def spread(q, row):
        pieces = []
        token_block = lax.broadcasted_iota(jnp.int32, (1, 2 * rows), 1) // rows
        for xx in range(NX):
            both = jnp.concatenate(
                [met[2 * q, z, pl.ds(row + xx, 1), :], met[2 * q + 1, z, pl.ds(row + xx, 1), :]], axis=1
            )
            for h in range(2):
                pieces.append(jnp.where(token_block == h, both, 0.0))
        return pieces

    slot_of = lax.broadcasted_iota(jnp.int32, (CAP, 2 * rows), 0).astype(f32) + 1.0
    pair_rows = 2 * CAP

    def gather(q):
        pick = jnp.concatenate([(line == slot_of).astype(f32) for line in spread(q, 0)], axis=0).astype(bf16)

        @pl.loop(0, width // 256)
        def _(n):
            cols = pl.ds(pl.multiple_of(n * 256, 256), 256)
            pair = tok[pl.ds(2 * q, 2), :, cols].reshape(2 * rows, 256)
            got = jnp.dot(pick, pair, preferred_element_type=f32).astype(bf16)
            for xx in range(NX):
                xs[q, xx, :, cols] = got[xx * pair_rows : (xx + 1) * pair_rows]

        for j in range(1, NX):
            to = (x + j) % NX
            remote(xs.at[q, to], xr.at[q, x], xd_s.at[q, j], xd_r.at[q, j], at_x(to)).start()
        xr[q, x] = xs[q, x]

    def expert(q):
        for j in range(1, NX):
            src = (x + NX - j) % NX
            remote(xs.at[q, src], xr.at[q, src], xd_s.at[q, j], xd_r.at[q, j], at_x(src)).wait_recv()
        row_in = xr[q].reshape(NX * pair_rows, width)

        @pl.loop(0, ff // 256)
        def _(n):
            at_gate = pl.ds(pl.multiple_of(n * 256, 256), 256)
            at_up = pl.ds(pl.multiple_of(ff + n * 256, 256), 256)
            gate = jnp.dot(row_in, wgu[:, at_gate], preferred_element_type=f32)
            upper = jnp.dot(row_in, wgu[:, at_up], preferred_element_type=f32)
            hid[:, at_gate] = (jnp.maximum(gate, 0.0) * upper).astype(bf16)

        hidden = hid[...]

        @pl.loop(0, width // 256)
        def _(n):
            cols = pl.ds(pl.multiple_of(n * 256, 256), 256)
            got = jnp.dot(hidden, wdn[:, cols], preferred_element_type=f32).astype(bf16)
            for xx in range(NX):
                ys[q, xx, :, cols] = got[xx * pair_rows : (xx + 1) * pair_rows]

        for j in range(1, NX):
            to = (x + j) % NX
            remote(ys.at[q, to], yr.at[q, x], xb_s.at[q, j], xb_r.at[q, j], at_x(to)).start()
        yr[q, x] = ys[q, x]

    def mix(q):
        for j in range(1, NX):
            src = (x + NX - j) % NX
            remote(ys.at[q, src], yr.at[q, src], xb_s.at[q, j], xb_r.at[q, j], at_x(src)).wait_recv()
        weigh = jnp.concatenate(
            [
                jnp.where(line == slot_of, gate, 0.0)
                for line, gate in zip(spread(q, 0), spread(q, NX))
            ],
            axis=0,
        )
        high = weigh.astype(bf16)
        low = (weigh - high.astype(f32)).astype(bf16)
        high, low = high.T, low.T

        @pl.loop(0, width // 256)
        def _(n):
            cols = pl.ds(pl.multiple_of(n * 256, 256), 256)
            back = yr[q, :, :, cols].reshape(NX * pair_rows, 256)
            total = jnp.dot(high, back, preferred_element_type=f32) + jnp.dot(
                low, back, preferred_element_type=f32
            )
            part[pl.ds(2 * q, 2), :, cols] = total.reshape(2, rows, 256)

    rs_piece = rows // RS_PIECES

    def add_and_send(s, rin, rs_r, first, to):
        for p in range(RS_PIECES):
            at = pl.ds(p * rs_piece, rs_piece)
            copy = remote(rout.at[s, at], rin.at[s, at], rs_s.at[s, p], rs_r.at[s, p], at_z(to))

            @pl.when(first)
            def _():
                rout[s, at] = part[s, at].astype(bf16)

            @pl.when(jnp.logical_not(first))
            def _():
                copy.wait_recv()
                rout[s, at] = (part[s, at] + rin[s, at].astype(f32)).astype(bf16)

            copy.start()

    def step(d, carry):
        @pl.when(jnp.logical_and(d < NZ, z >= d))
        def _():
            got = block_to(0, z - d, d, jnp.minimum(z + 1, NZ - 1))
            send = block_to(0, z - d, d + 1, jnp.minimum(z + 1, NZ - 1))
            for one, two in zip(got, send):
                one.wait_recv()

                @pl.when(z < NZ - 1)
                def _():
                    two.start()

        @pl.when(jnp.logical_and(d < NZ, z + d <= NZ - 1))
        def _():
            got = block_to(1, z + d, d, jnp.maximum(z - 1, 0))
            send = block_to(1, z + d, d + 1, jnp.maximum(z - 1, 0))
            for one, two in zip(got, send):
                one.wait_recv()

                @pl.when(z > 0)
                def _():
                    two.start()

        @pl.when(d == 2)
        def _():
            wait_recv(hop2)
            start(mate_up)
            start(mate_dn)
            start(to_core[4])
            wait_recv(far_own_in)
            start(to_core[3])

        @pl.when(d == 3)
        def _():
            wait_recv(mate_from_up)
            start(far_mate)
            start(to_core[6])
            wait_recv(mate_from_dn)
            start(to_core[5])

        @pl.when(d == 4)
        def _():
            wait_recv(far_mate_in)
            start(to_core[7])

        q, valid = pair_at(d)

        @pl.when(valid)
        def _():
            gather(q)

        @pl.when(d == WEIGHTS_AT)
        def _():
            for copies in of_core:
                wait_recv(copies)

        q_e, valid_e = pair_at(d - LAG_EXPERT)

        @pl.when(valid_e)
        def _():
            expert(q_e)

        q_m, valid_m = pair_at(d - LAG_MIX)

        @pl.when(valid_m)
        def _():
            mix(q_m)

        s_b = NZ - 1 + LAG_SUM - d

        @pl.when(jnp.logical_and(s_b >= 0, s_b < z))
        def _():
            add_and_send(s_b, rin_b, rs_rb, z == NZ - 1, z - 1)

        s_f = d - LAG_SUM

        @pl.when(jnp.logical_and(s_f > z, s_f <= NZ - 1))
        def _():
            add_and_send(s_f, rin_f, rs_rf, z == 0, z + 1)

        return carry

    lax.fori_loop(1, STEPS + 1, step, 0)

    for p in range(RS_PIECES):
        at = pl.ds(p * rs_piece, rs_piece)

        @pl.when(z < NZ - 1)
        def _():
            remote(rout.at[z, at], rin_b.at[z, at], rs_s.at[z, p], rs_rb.at[z, p], at_z(z + 1)).wait_recv()
            part[z, at] = part[z, at] + rin_b[z, at].astype(f32)

        @pl.when(z > 0)
        def _():
            remote(rout.at[z, at], rin_f.at[z, at], rs_s.at[z, p], rs_rf.at[z, p], at_z(z - 1)).wait_recv()
            part[z, at] = part[z, at] + rin_f[z, at].astype(f32)

        out[at, :] = part[z, at].astype(bf16)

    wait_send(hop1 + hop2 + mine_up + mine_dn + mate_up + mate_dn + far_own + far_mate)
    for copies in to_core:
        wait_send(copies)

    def drain(d, carry):
        @pl.when(jnp.logical_and(z < NZ - 1, z >= d - 1))
        def _():
            wait_send(block_to(0, z - d + 1, d, z + 1))

        @pl.when(jnp.logical_and(z > 0, z + d - 1 <= NZ - 1))
        def _():
            wait_send(block_to(1, z + d - 1, d, z - 1))

        return carry

    lax.fori_loop(1, NZ, drain, 0)

    def drain_pair(q, carry):
        for j in range(1, NX):
            to = (x + j) % NX
            remote(xs.at[q, to], xr.at[q, x], xd_s.at[q, j], xd_r.at[q, j], at_x(to)).wait_send()
            remote(ys.at[q, to], yr.at[q, x], xb_s.at[q, j], xb_r.at[q, j], at_x(to)).wait_send()
        return carry

    lax.fori_loop(0, NZ // 2, drain_pair, 0)

    def drain_sum(s, carry):
        @pl.when(s != z)
        def _():
            for p in range(RS_PIECES):
                at = pl.ds(p * rs_piece, rs_piece)
                remote(
                    rout.at[s, at], rin_b.at[s, at], rs_s.at[s, p], rs_rb.at[s, p],
                    at_z(jnp.where(s < z, z - 1, z + 1)),
                ).wait_send()

        return carry

    lax.fori_loop(0, NZ, drain_sum, 0)


def on_device(
    tokens, norm_gain, router_weight, routes, placement, gate_weight, up_weight, down_weight
):
    rows, width = tokens.shape
    experts = router_weight.shape[1]
    ff = gate_weight.shape[2]
    grows, drows = gate_weight.shape[1], down_weight.shape[1]
    blks = lax.axis_size("blk")
    bf16, f32 = jnp.bfloat16, jnp.float32
    dma = pltpu.SemaphoreType.DMA
    vmem = pl.BlockSpec(memory_space=pltpu.VMEM)
    hbm = pl.BlockSpec(memory_space=pl.ANY)
    rows_of = (NZ // 2, NX, 2 * CAP, width)
    return pl.pallas_call(
        kernel,
        out_shape=jax.ShapeDtypeStruct((rows, width), bf16),
        in_specs=[vmem] * 5 + [hbm] * 3,
        out_specs=vmem,
        scratch_shapes=[
            pltpu.VMEM((NZ, rows, width), bf16),
            pltpu.VMEM((NZ, NZ, 2 * NX, rows), f32),
            pltpu.VMEM((blks * grows, 2 * ff), bf16),
            pltpu.VMEM((blks * drows, width), bf16),
            pltpu.VMEM((2, grows // 2, 2 * ff), bf16),
            pltpu.VMEM((2, drows, width // 2), bf16),
            pltpu.VMEM(rows_of, bf16),
            pltpu.VMEM(rows_of, bf16),
            pltpu.VMEM(rows_of, bf16),
            pltpu.VMEM(rows_of, bf16),
            pltpu.VMEM((NX * 2 * CAP, ff), bf16),
            pltpu.VMEM((NZ, rows, width), f32),
            pltpu.VMEM((NZ, rows, width), bf16),
            pltpu.VMEM((NZ, rows, width), bf16),
            pltpu.VMEM((NZ, rows, width), bf16),
            dma((3,)),
            dma((2, 2, 2)), dma((2, 2, 2)),
            dma((2, 2)), dma((2, 2)), dma((2, 2)), dma((2, 2)), dma((2, 2)), dma((2, 2)),
            dma((8, 2)), dma((8, 2)),
            dma((2, NZ + 1, AG_PIECES)), dma((2, NZ + 1, AG_PIECES)),
            dma((2, NZ + 1)), dma((2, NZ + 1)),
            dma((NZ // 2, NX)), dma((NZ // 2, NX)), dma((NZ // 2, NX)), dma((NZ // 2, NX)),
            dma((NZ, RS_PIECES)), dma((NZ, RS_PIECES)), dma((NZ, RS_PIECES)),
        ],
        compiler_params=pltpu.CompilerParams(
            collective_id=0, has_side_effects=True, vmem_limit_bytes=60 * 1024 * 1024
        ),
    )(
        tokens,
        norm_gain.reshape(1, width),
        routes.T,
        router_weight.T,
        placement.reshape(1, experts),
        gate_weight[0],
        up_weight[0],
        down_weight[0],
    )


def solution(mesh):
    in_specs = (
        P(("ep", "blk"), None),
        P(),
        P(),
        P(("ep", "blk"), None),
        P(),
        P("ep", "blk", None),
        P("ep", "blk", None),
        P("ep", "blk", None),
    )
    out_specs = P(("ep", "blk"), None)
    return jax.shard_map(
        on_device, mesh=mesh, in_specs=in_specs, out_specs=out_specs, check_vma=False
    )
```

time: 484 us -> 263 us (0.54)
  the two profiles are of different devices: /device:TPU:1 before, /device:TPU:240 now
where the time goes in v1:
time: 263 us
  Pallas kernels  260 us (99%)
  local copies, waits for them, and re-layouts  3.05 us (1%)
    pallas_call x1, Pallas kernels, on_device(): pl.pallas_call(kernel, out_shape=jax.ShapeDtypeStruct((rows, width), bf16...  260 us

profile of v1, /device:TPU:240, one launch (start us, length us, event | category | flops | bytes accessed | tf_op | source)
XLA Modules:
  0.0 262.6 jit_solution(2015314254862559537)
XLA Ops:
  0.0 0.0 copy-start
  0.0 0.7 copy-done
  0.7 0.6 reshape.6.gain
  1.3 259.5 %shard_map.82 = bf16[128,1536]{1,0:T(8,128)(2,1)} custom-call(bf16[128,1536]{1,0:T(8,128)(2,1)} %tokens.1, bf16[1,1536]{1,0:T(2,128)(2,1)} %reshape.6.gain, s32[4,128]{1,0:T(4,128)} %bitcast.10, bf16[32,1536]{1,0:T(8,128)(2,1)} %bitcast.9, s32[1,32]{1,0:T(1,128)} %bitcast.11, bf16[96,768]{1,0:T(8,128)(2,1)} %bitcast.6, bf16[96,768]{1,0:T(8,128)(2,1)} %bitcast.7, ...), custom_call_target="tpu_custom_call" | custom-call | tf_op jit(solution)/shard_map/pallas_call | solution.py:469
  260.8 1.8 copy.10
Async XLA Ops:
  0.0 0.7 copy-start

commit v2 on v1

--- a/solution.py
+++ b/solution.py
@@ -10,19 +10,22 @@
 MESH = pl.DeviceIdType.MESH
 NZ, NX, NY = 8, 4, 4
 CAP = 24
-LAG_EXPERT = 4
-LAG_MIX = 5
-LAG_SUM = 6
-STEPS = NZ - 1 + LAG_SUM
-WEIGHTS_AT = 5
-AG_PIECES = 2
-RS_PIECES = 4
+PIECES = 4
+LAG_EXPERT = 6
+LAG_MIX = 12
+LAG_SUM = 2 * PIECES + LAG_MIX
+HOP = 7
+TICKS = (NZ - 1) * PIECES + ((NZ - 1) * HOP + 3) // 4 + LAG_SUM + 4
+MATE_AT = (2, 5, 9)
+OWN_ROWS_AT = 4
+MATE_ROWS_AT = (8, 11, 13)
+WEIGHTS_AT = 2 * PIECES - 1 + LAG_EXPERT
 
 
 def kernel(
     tokens, gain, routes_t, router_t, placement, gate_w, up_w, down_w, out,
-    tok, met, wgu, wdn, rel_gu, rel_dn, xs, xr, ys, yr, hid, part, rin_b, rin_f, rout,
-    loc_sem, z_s, z_r, yo_s, yo_r, yp_s, yp_r, y2_s, y2_r, c_s, c_r,
+    tok, met, wgu, wdn, xs, xr, ys, yr, hid, part, rin_b, rin_f, rout,
+    loc_sem, z_s, z_r, yo_s, yo_r, yp_s, yp_r, co_s, co_r, cp_s, cp_r,
     ag_s, ag_r, mg_s, mg_r, xd_s, xd_r, xb_s, xb_r, rs_s, rs_rb, rs_rf,
 ):
     f32, bf16 = jnp.float32, jnp.bfloat16
@@ -40,15 +43,13 @@
     def at_z(zz):
         return {"ep": zz * NX + x, "blk": blk}
 
+    def at_y(j):
+        return {"ep": ep, "blk": blk_of(y + j, zh, c)}
+
     def at_x(xx):
         return {"ep": z * NX + xx, "blk": blk}
 
-    up4 = {"ep": ((z + 4) % NZ) * NX + x, "blk": blk_of(y, (zh + z // 4) % 2, c)}
-    dn4_zh = (zh + 1 - z // 4) % 2
-    dn4 = {"ep": ((z + 4) % NZ) * NX + x, "blk": blk_of(y, dn4_zh, c)}
-    up4_zh = (zh + z // 4) % 2
-    y_up = {"ep": ep, "blk": blk_of(y + 1, zh, c)}
-    y_dn = {"ep": ep, "blk": blk_of(y - 1, zh, c)}
+    mate = {"ep": ep, "blk": blk_of(y, 1 - zh, c)}
     core = {"ep": ep, "blk": blk_of(y, zh, 1 - c)}
 
     def remote(src, dst, s, r, dev):
@@ -76,8 +77,10 @@
     def greet(dev):
         pl.semaphore_signal(barrier, inc=1, device_id=dev, device_id_type=MESH)
 
-    for dev in (up4, dn4, y_up, y_dn, core):
-        greet(dev)
+    greet(mate)
+    greet(core)
+    for j in range(1, NY):
+        greet(at_y(j))
     for j in range(1, NX):
         greet(at_x((x + j) % NX))
 
@@ -95,64 +98,76 @@
     for copy in local:
         copy.wait()
 
-    half_g, half_d = grows // 2, width // 2
-
-    def gu_half(b, h):
-        return wgu.at[pl.ds(pl.multiple_of(b * grows + h * half_g, half_g), half_g)]
-
-    def dn_half(b, h):
-        return wdn.at[pl.ds(pl.multiple_of(b * drows, drows), drows), pl.ds(h * half_d, half_d)]
-
-    hop1, hop2 = [], []
-    for h, dev, owner in ((0, up4, blk_of(y, dn4_zh, c)), (1, dn4, blk_of(y, up4_zh, c))):
-        hop1 += [
-            remote(gu_half(blk, h), rel_gu.at[h], z_s.at[0, h, 0], z_r.at[0, h, 0], dev),
-            remote(dn_half(blk, h), rel_dn.at[h], z_s.at[0, h, 1], z_r.at[0, h, 1], dev),
+    half_g = grows // 2
+
+    def part_at(b, p):
+        if p == 2:
+            return dn_at(b)
+        return wgu.at[pl.ds(pl.multiple_of(b * grows + p * half_g, half_g), half_g)]
+
+    def part_to(b, p, s, r, dev):
+        return remote(part_at(b, p), part_at(b, p), s, r, dev)
+
+    parts = range(3)
+    mate_blk = blk_of(y, 1 - zh, c)
+    mate_out = [part_to(blk, p, z_s.at[p], z_r.at[p], mate) for p in parts]
+    mate_in = [part_to(mate_blk, p, z_s.at[p], z_r.at[p], mate) for p in parts]
+
+    def y_copies(zz, s, r, far):
+        return [
+            [
+                part_to(blk_of(y - j, zz, c) if far else blk_of(y, zz, c), p, s.at[j, p], r.at[j, p], at_y(j))
+                for p in parts
+            ]
+            for j in range(NY)
         ]
-        hop2 += [
-            remote(rel_gu.at[h], gu_half(owner, h), z_s.at[1, h, 0], z_r.at[1, h, 0], dev),
-            remote(rel_dn.at[h], dn_half(owner, h), z_s.at[1, h, 1], z_r.at[1, h, 1], dev),
+
+    def core_copies(zz, cc, s, r):
+        return [
+            [part_to(blk_of(y - j, zz, cc), p, s.at[j, p], r.at[j, p], core) for p in parts]
+            for j in range(NY)
         ]
-    mate = blk_of(y, 1 - zh, c)
-
-    def shard_to(b, s, r, dev):
-        return [
-            remote(gu_at(b), gu_at(b), s.at[0], r.at[0], dev),
-            remote(dn_at(b), dn_at(b), s.at[1], r.at[1], dev),
-        ]
-
-    def start(copies):
-        for copy in copies:
-            copy.start()
-
-    def wait_recv(copies):
-        for copy in copies:
-            copy.wait_recv()
-
-    def wait_send(copies):
-        for copy in copies:
-            copy.wait_send()
-
-    mine_up = shard_to(blk, yo_s.at[0], yo_r.at[0], y_up)
-    mine_dn = shard_to(blk, yo_s.at[1], yo_r.at[1], y_dn)
-    from_dn = shard_to(blk_of(y - 1, zh, c), yo_s.at[0], yo_r.at[0], y_dn)
-    from_up = shard_to(blk_of(y + 1, zh, c), yo_s.at[1], yo_r.at[1], y_up)
-    mate_up = shard_to(mate, yp_s.at[0], yp_r.at[0], y_up)
-    mate_dn = shard_to(mate, yp_s.at[1], yp_r.at[1], y_dn)
-    mate_from_dn = shard_to(blk_of(y - 1, 1 - zh, c), yp_s.at[0], yp_r.at[0], y_dn)
-    mate_from_up = shard_to(blk_of(y + 1, 1 - zh, c), yp_s.at[1], yp_r.at[1], y_up)
-    far_own = shard_to(blk_of(y - 1, zh, c), y2_s.at[0], y2_r.at[0], y_up)
-    far_mate = shard_to(blk_of(y + 1, 1 - zh, c), y2_s.at[1], y2_r.at[1], y_dn)
-    far_own_in = shard_to(blk_of(y - 2, zh, c), y2_s.at[0], y2_r.at[0], y_dn)
-    far_mate_in = shard_to(blk_of(y + 2, 1 - zh, c), y2_s.at[1], y2_r.at[1], y_up)
-    held = [(0, zh), (-1, zh), (1, zh), (2, zh), (0, 1 - zh), (-1, 1 - zh), (1, 1 - zh), (2, 1 - zh)]
-    to_core = [shard_to(blk_of(y + dy, zz, c), c_s.at[k], c_r.at[k], core) for k, (dy, zz) in enumerate(held)]
-    of_core = [shard_to(blk_of(y + dy, zz, 1 - c), c_s.at[k], c_r.at[k], core) for k, (dy, zz) in enumerate(held)]
-
-    start(hop1)
-    start(mine_up)
-    start(mine_dn)
-    start(to_core[0])
+
+    own_out, own_in = y_copies(zh, yo_s, yo_r, False), y_copies(zh, yo_s, yo_r, True)
+    pass_out, pass_in = y_copies(1 - zh, yp_s, yp_r, False), y_copies(1 - zh, yp_s, yp_r, True)
+    own_core, own_of_core = core_copies(zh, c, co_s, co_r), core_copies(zh, 1 - c, co_s, co_r)
+    mate_core, mate_of_core = core_copies(1 - zh, c, cp_s, cp_r), core_copies(1 - zh, 1 - c, cp_s, cp_r)
+
+    for copy in mate_out:
+        copy.start()
+    for p in parts:
+        for j in (1, 3, 2):
+            own_out[j][p].start()
+        own_core[0][p].start()
+
+    def weights_at(t):
+        for p in parts:
+            @pl.when(t == MATE_AT[p])
+            def _():
+                mate_in[p].wait_recv()
+                for j in (1, 3, 2):
+                    pass_out[j][p].start()
+                mate_core[0][p].start()
+
+        @pl.when(t == OWN_ROWS_AT)
+        def _():
+            for p in parts:
+                for j in (1, 3, 2):
+                    own_in[j][p].wait_recv()
+                    own_core[j][p].start()
+
+        for p in parts:
+            @pl.when(t == MATE_ROWS_AT[p])
+            def _():
+                for j in (1, 3, 2):
+                    pass_in[j][p].wait_recv()
+                    mate_core[j][p].start()
+
+        @pl.when(t == WEIGHTS_AT)
+        def _():
+            for copies in own_of_core + mate_of_core:
+                for copy in copies:
+                    copy.wait_recv()
 
     values = tokens[...].astype(f32)
     square = jnp.mean(values * values, axis=-1, keepdims=True)
@@ -181,37 +196,57 @@
         met[z, zz, pl.ds(0, NX), :] = slot[zz * NX : (zz + 1) * NX]
         met[z, zz, pl.ds(NX, NX), :] = gates[zz * NX : (zz + 1) * NX]
 
-    piece = rows // AG_PIECES
-
-    def block_to(way, s, d, zz):
-        copies = [remote(met.at[s], met.at[s], mg_s.at[way, d], mg_r.at[way, d], at_z(zz))]
-        for p in range(AG_PIECES):
-            part_of = tok.at[s, pl.ds(p * piece, piece)]
-            copies.append(remote(part_of, part_of, ag_s.at[way, d, p], ag_r.at[way, d, p], at_z(zz)))
-        return copies
-
-    @pl.when(z < NZ - 1)
-    def _():
-        start(block_to(0, z, 1, z + 1))
-
-    @pl.when(z > 0)
-    def _():
-        start(block_to(1, z, 1, z - 1))
-
-    for one, two in zip(hop1, hop2):
-        one.wait_recv()
-        two.start()
-    wait_recv(from_dn)
-    start(far_own)
-    start(to_core[1])
-    wait_recv(from_up)
-    start(to_core[2])
-
-    def pair_at(d):
-        left = (z + d) % 2 == 0
-        q = jnp.where(left, (z - d) // 2, (z + d - 1) // 2)
-        valid = jnp.logical_and(d >= 1, jnp.where(left, z - d >= 0, z + d - 1 <= NZ - 1))
-        return jnp.where(valid, q, 0), valid
+    piece = rows // PIECES
+    last = NZ - 1
+    behind_up = jnp.maximum(0, ((2 * z - last) * HOP + 3) // 4)
+    behind_down = jnp.maximum(0, ((last - 2 * z) * HOP + 3) // 4)
+
+    def piece_at(p):
+        return pl.ds(pl.multiple_of(p * piece, piece), piece)
+
+    def piece_to(way, s, p, zz):
+        part_of = tok.at[s, piece_at(p)]
+        return remote(part_of, part_of, ag_s.at[way, s, p], ag_r.at[s, p], at_z(zz))
+
+    def table_to(way, s, zz):
+        return remote(met.at[s], met.at[s], mg_s.at[way, s], mg_r.at[s], at_z(zz))
+
+    def relay(way, k):
+        t, p = k // PIECES, k % PIECES
+        s = t if way == 0 else last - t
+        inside = jnp.logical_and(k >= 0, t < NZ)
+        comes = jnp.logical_and(inside, s < z if way == 0 else s > z)
+        goes = jnp.logical_and(s <= z, z < last) if way == 0 else jnp.logical_and(s >= z, z > 0)
+        goes = jnp.logical_and(inside, goes)
+        to = jnp.minimum(z + 1, last) if way == 0 else jnp.maximum(z - 1, 0)
+
+        @pl.when(jnp.logical_and(comes, p == 0))
+        def _():
+            table_to(way, s, to).wait_recv()
+
+        @pl.when(jnp.logical_and(goes, p == 0))
+        def _():
+            table_to(way, s, to).start()
+
+        @pl.when(comes)
+        def _():
+            piece_to(way, s, p, to).wait_recv()
+
+        @pl.when(goes)
+        def _():
+            piece_to(way, s, p, to).start()
+
+    def pair_at(tick, way):
+        k = tick - jnp.where(way == 0, behind_up, behind_down)
+        t = k // PIECES
+        whole = jnp.logical_and(jnp.logical_and(k >= 0, t < NZ), k % PIECES == PIECES - 1)
+        s = jnp.where(way == 0, t, last - t)
+        odd = t % 2 == 1
+        passed = jnp.logical_and(odd, jnp.where(way == 0, s < z, s > z))
+        own_t = jnp.maximum(1, jnp.where(way == 0, z - 1, last - 1 - z))
+        own = jnp.logical_and(z % 2 == 1 - way, t == own_t)
+        valid = jnp.logical_and(whole, jnp.logical_or(passed, own))
+        return jnp.where(valid, jnp.where(own, z // 2, s // 2), 0), valid
 
     def spread(q, row):
         pieces = []
@@ -295,11 +330,17 @@
             )
             part[pl.ds(2 * q, 2), :, cols] = total.reshape(2, rows, 256)
 
-    rs_piece = rows // RS_PIECES
-
-    def add_and_send(s, rin, rs_r, first, to):
-        for p in range(RS_PIECES):
-            at = pl.ds(p * rs_piece, rs_piece)
+    def add_and_send(way, k):
+        r, p = k // PIECES, k % PIECES
+        s = r if way == 0 else last - r
+        inside = jnp.logical_and(k >= 0, r < NZ)
+        rin, rs_r = (rin_b, rs_rb) if way == 0 else (rin_f, rs_rf)
+        first = z == (last if way == 0 else 0)
+        to = jnp.maximum(z - 1, 0) if way == 0 else jnp.minimum(z + 1, last)
+
+        @pl.when(jnp.logical_and(inside, s < z if way == 0 else s > z))
+        def _():
+            at = piece_at(p)
             copy = remote(rout.at[s, at], rin.at[s, at], rs_s.at[s, p], rs_r.at[s, p], at_z(to))
 
             @pl.when(first)
@@ -313,92 +354,36 @@
 
             copy.start()
 
-    def step(d, carry):
-        @pl.when(jnp.logical_and(d < NZ, z >= d))
-        def _():
-            got = block_to(0, z - d, d, jnp.minimum(z + 1, NZ - 1))
-            send = block_to(0, z - d, d + 1, jnp.minimum(z + 1, NZ - 1))
-            for one, two in zip(got, send):
-                one.wait_recv()
-
-                @pl.when(z < NZ - 1)
-                def _():
-                    two.start()
-
-        @pl.when(jnp.logical_and(d < NZ, z + d <= NZ - 1))
-        def _():
-            got = block_to(1, z + d, d, jnp.maximum(z - 1, 0))
-            send = block_to(1, z + d, d + 1, jnp.maximum(z - 1, 0))
-            for one, two in zip(got, send):
-                one.wait_recv()
-
-                @pl.when(z > 0)
-                def _():
-                    two.start()
-
-        @pl.when(d == 2)
-        def _():
-            wait_recv(hop2)
-            start(mate_up)
-            start(mate_dn)
-            start(to_core[4])
-            wait_recv(far_own_in)
-            start(to_core[3])
-
-        @pl.when(d == 3)
-        def _():
-            wait_recv(mate_from_up)
-            start(far_mate)
-            start(to_core[6])
-            wait_recv(mate_from_dn)
-            start(to_core[5])
-
-        @pl.when(d == 4)
-        def _():
-            wait_recv(far_mate_in)
-            start(to_core[7])
-
-        q, valid = pair_at(d)
-
-        @pl.when(valid)
-        def _():
-            gather(q)
-
-        @pl.when(d == WEIGHTS_AT)
-        def _():
-            for copies in of_core:
-                wait_recv(copies)
-
-        q_e, valid_e = pair_at(d - LAG_EXPERT)
-
-        @pl.when(valid_e)
-        def _():
-            expert(q_e)
-
-        q_m, valid_m = pair_at(d - LAG_MIX)
-
-        @pl.when(valid_m)
-        def _():
-            mix(q_m)
-
-        s_b = NZ - 1 + LAG_SUM - d
-
-        @pl.when(jnp.logical_and(s_b >= 0, s_b < z))
-        def _():
-            add_and_send(s_b, rin_b, rs_rb, z == NZ - 1, z - 1)
-
-        s_f = d - LAG_SUM
-
-        @pl.when(jnp.logical_and(s_f > z, s_f <= NZ - 1))
-        def _():
-            add_and_send(s_f, rin_f, rs_rf, z == 0, z + 1)
-
+    def stage(work, tick):
+        def one(way, carry):
+            q, valid = pair_at(tick, way)
+
+            @pl.when(valid)
+            def _():
+                work(q)
+
+            return carry
+
+        lax.fori_loop(0, 2, one, 0)
+
+    sum_down_at = behind_up + LAG_SUM + ((last - z) * 2 * HOP + 3) // 4
+    sum_up_at = behind_down + LAG_SUM + (z * 2 * HOP + 3) // 4
+
+    def step(tick, carry):
+        weights_at(tick)
+        relay(0, tick - behind_up)
+        relay(1, tick - behind_down)
+        stage(gather, tick)
+        stage(expert, tick - LAG_EXPERT)
+        stage(mix, tick - LAG_MIX)
+        add_and_send(0, tick - sum_down_at)
+        add_and_send(1, tick - sum_up_at)
         return carry
 
-    lax.fori_loop(1, STEPS + 1, step, 0)
-
-    for p in range(RS_PIECES):
-        at = pl.ds(p * rs_piece, rs_piece)
+    lax.fori_loop(0, TICKS, step, 0)
+
+    for p in range(PIECES):
+        at = pl.ds(p * piece, piece)
 
         @pl.when(z < NZ - 1)
         def _():
@@ -412,22 +397,31 @@
 
         out[at, :] = part[z, at].astype(bf16)
 
-    wait_send(hop1 + hop2 + mine_up + mine_dn + mate_up + mate_dn + far_own + far_mate)
-    for copies in to_core:
-        wait_send(copies)
-
-    def drain(d, carry):
-        @pl.when(jnp.logical_and(z < NZ - 1, z >= d - 1))
-        def _():
-            wait_send(block_to(0, z - d + 1, d, z + 1))
-
-        @pl.when(jnp.logical_and(z > 0, z + d - 1 <= NZ - 1))
-        def _():
-            wait_send(block_to(1, z + d - 1, d, z - 1))
+    for p in parts:
+        mate_out[p].wait_send()
+        for j in range(NY):
+            if j:
+                own_out[j][p].wait_send()
+                pass_out[j][p].wait_send()
+            own_core[j][p].wait_send()
+            mate_core[j][p].wait_send()
+
+    def drain(s, carry):
+        @pl.when(jnp.logical_and(s <= z, z < NZ - 1))
+        def _():
+            table_to(0, s, z + 1).wait_send()
+            for p in range(PIECES):
+                piece_to(0, s, p, z + 1).wait_send()
+
+        @pl.when(jnp.logical_and(s >= z, z > 0))
+        def _():
+            table_to(1, s, z - 1).wait_send()
+            for p in range(PIECES):
+                piece_to(1, s, p, z - 1).wait_send()
 
         return carry
 
-    lax.fori_loop(1, NZ, drain, 0)
+    lax.fori_loop(0, NZ, drain, 0)
 
     def drain_pair(q, carry):
         for j in range(1, NX):
@@ -441,8 +435,8 @@
     def drain_sum(s, carry):
         @pl.when(s != z)
         def _():
-            for p in range(RS_PIECES):
-                at = pl.ds(p * rs_piece, rs_piece)
+            for p in range(PIECES):
+                at = pl.ds(p * piece, piece)
                 remote(
                     rout.at[s, at], rin_b.at[s, at], rs_s.at[s, p], rs_rb.at[s, p],
                     at_z(jnp.where(s < z, z - 1, z + 1)),
@@ -476,8 +470,6 @@
             pltpu.VMEM((NZ, NZ, 2 * NX, rows), f32),
             pltpu.VMEM((blks * grows, 2 * ff), bf16),
             pltpu.VMEM((blks * drows, width), bf16),
-            pltpu.VMEM((2, grows // 2, 2 * ff), bf16),
-            pltpu.VMEM((2, drows, width // 2), bf16),
             pltpu.VMEM(rows_of, bf16),
             pltpu.VMEM(rows_of, bf16),
             pltpu.VMEM(rows_of, bf16),
@@ -488,13 +480,13 @@
             pltpu.VMEM((NZ, rows, width), bf16),
             pltpu.VMEM((NZ, rows, width), bf16),
             dma((3,)),
-            dma((2, 2, 2)), dma((2, 2, 2)),
-            dma((2, 2)), dma((2, 2)), dma((2, 2)), dma((2, 2)), dma((2, 2)), dma((2, 2)),
-            dma((8, 2)), dma((8, 2)),
-            dma((2, NZ + 1, AG_PIECES)), dma((2, NZ + 1, AG_PIECES)),
-            dma((2, NZ + 1)), dma((2, NZ + 1)),
+            dma((3,)), dma((3,)),
+            dma((NY, 3)), dma((NY, 3)), dma((NY, 3)), dma((NY, 3)),
+            dma((NY, 3)), dma((NY, 3)), dma((NY, 3)), dma((NY, 3)),
+            dma((2, NZ, PIECES)), dma((NZ, PIECES)),
+            dma((2, NZ)), dma((NZ,)),
             dma((NZ // 2, NX)), dma((NZ // 2, NX)), dma((NZ // 2, NX)), dma((NZ // 2, NX)),
-            dma((NZ, RS_PIECES)), dma((NZ, RS_PIECES)), dma((NZ, RS_PIECES)),
+            dma((NZ, PIECES)), dma((NZ, PIECES)), dma((NZ, PIECES)),
         ],
         compiler_params=pltpu.CompilerParams(
             collective_id=0, has_side_effects=True, vmem_limit_bytes=60 * 1024 * 1024

time: 263 us -> 205 us (0.78)
  the two profiles are of different devices: /device:TPU:240 before, /device:TPU:134 now
where the time goes in v2:
time: 205 us
  Pallas kernels  202 us (99%)
  local copies, waits for them, and re-layouts  3.05 us (1%)
    pallas_call x1, Pallas kernels, on_device(): pl.pallas_call(kernel, out_shape=jax.ShapeDtypeStruct((rows, width), bf16...  202 us

profile of v2, /device:TPU:134, one launch (start us, length us, event | category | flops | bytes accessed | tf_op | source)
XLA Modules:
  0.0 205.2 jit_solution(4966245260150991076)
XLA Ops:
  0.0 0.0 copy-start
  0.0 0.7 copy-done
  0.7 0.6 reshape.6.gain
  1.3 202.2 %shard_map.82 = bf16[128,1536]{1,0:T(8,128)(2,1)} custom-call(bf16[128,1536]{1,0:T(8,128)(2,1)} %tokens.1, bf16[1,1536]{1,0:T(2,128)(2,1)} %reshape.6.gain, s32[4,128]{1,0:T(4,128)} %bitcast.10, bf16[32,1536]{1,0:T(8,128)(2,1)} %bitcast.9, s32[1,32]{1,0:T(1,128)} %bitcast.11, bf16[96,768]{1,0:T(8,128)(2,1)} %bitcast.6, bf16[96,768]{1,0:T(8,128)(2,1)} %bitcast.7, ...), custom_call_target="tpu_custom_call" | custom-call | tf_op jit(solution)/shard_map/pallas_call | solution.py:463
  203.5 1.8 copy.10
Async XLA Ops:
  0.0 0.7 copy-start

commit v3 on v2

--- a/solution.py
+++ b/solution.py
@@ -11,20 +11,22 @@
 NZ, NX, NY = 8, 4, 4
 CAP = 24
 PIECES = 4
-LAG_EXPERT = 6
-LAG_MIX = 12
-LAG_SUM = 2 * PIECES + LAG_MIX
-HOP = 7
-TICKS = (NZ - 1) * PIECES + ((NZ - 1) * HOP + 3) // 4 + LAG_SUM + 4
-MATE_AT = (2, 5, 9)
-OWN_ROWS_AT = 4
-MATE_ROWS_AT = (8, 11, 13)
-WEIGHTS_AT = 2 * PIECES - 1 + LAG_EXPERT
+LAG_EXPERT = 5
+LAG_MIX = 10
+MID_EXPERT = 2
+MID_MIX = 3
+HOP = 12
+SLOTS = 32
+TICKS = (NZ - 1) * PIECES + ((NZ - 1) * HOP + 3) // 4 + PIECES + LAG_MIX + 4
+MATE_AT = (4, 6, 9)
+MATE_START = (-1, -1, -1, -1, 0, 1, 2, 3, 4)
+OWN_ROWS_AT = 5
+MATE_ROWS_AT = (8, 10, 12)
 
 
 def kernel(
     tokens, gain, routes_t, router_t, placement, gate_w, up_w, down_w, out,
-    tok, met, wgu, wdn, xs, xr, ys, yr, hid, part, rin_b, rin_f, rout,
+    tok, met, named_by, router_p, wgu, wdn, xs, xr, ys, yr, hid, part, rin_b, rin_f, rout,
     loc_sem, z_s, z_r, yo_s, yo_r, yp_s, yp_r, co_s, co_r, cp_s, cp_r,
     ag_s, ag_r, mg_s, mg_r, xd_s, xd_r, xb_s, xb_r, rs_s, rs_rb, rs_rf,
 ):
@@ -108,10 +110,25 @@
     def part_to(b, p, s, r, dev):
         return remote(part_at(b, p), part_at(b, p), s, r, dev)
 
+    last = NZ - 1
+    middle = jnp.minimum(z, last - z)
+    behind_up = jnp.maximum(0, ((2 * z - last) * HOP + 3) // 4)
+    behind_down = jnp.maximum(0, ((last - 2 * z) * HOP + 3) // 4)
+    behind = jnp.maximum(behind_up, behind_down)
+
     parts = range(3)
     mate_blk = blk_of(y, 1 - zh, c)
-    mate_out = [part_to(blk, p, z_s.at[p], z_r.at[p], mate) for p in parts]
-    mate_in = [part_to(mate_blk, p, z_s.at[p], z_r.at[p], mate) for p in parts]
+
+    def third_at(b, p, i):
+        if p == 2:
+            return wdn.at[pl.ds(pl.multiple_of(b * drows + i * (drows // 3), drows // 3), drows // 3)]
+        return wgu.at[pl.ds(pl.multiple_of(b * grows + p * half_g + i * (half_g // 3), half_g // 3), half_g // 3)]
+
+    mate_out = [remote(third_at(blk, p, i), third_at(blk, p, i), z_s.at[p, i], z_r.at[p, i], mate) for p in parts for i in range(3)]
+    mate_in = [
+        [remote(third_at(mate_blk, p, i), third_at(mate_blk, p, i), z_s.at[p, i], z_r.at[p, i], mate) for i in range(3)]
+        for p in parts
+    ]
 
     def y_copies(zz, s, r, far):
         return [
@@ -133,18 +150,26 @@
     own_core, own_of_core = core_copies(zh, c, co_s, co_r), core_copies(zh, 1 - c, co_s, co_r)
     mate_core, mate_of_core = core_copies(1 - zh, c, cp_s, cp_r), core_copies(1 - zh, 1 - c, cp_s, cp_r)
 
-    for copy in mate_out:
-        copy.start()
+    for at, copy in zip(MATE_START, mate_out):
+        if at < 0:
+            copy.start()
     for p in parts:
         for j in (1, 3, 2):
             own_out[j][p].start()
         own_core[0][p].start()
 
     def weights_at(t):
+        for at, copy in zip(MATE_START, mate_out):
+            if at >= 0:
+                @pl.when(t == at)
+                def _():
+                    copy.start()
+
         for p in parts:
             @pl.when(t == MATE_AT[p])
             def _():
-                mate_in[p].wait_recv()
+                for copy in mate_in[p]:
+                    copy.wait_recv()
                 for j in (1, 3, 2):
                     pass_out[j][p].start()
                 mate_core[0][p].start()
@@ -163,7 +188,7 @@
                     pass_in[j][p].wait_recv()
                     mate_core[j][p].start()
 
-        @pl.when(t == WEIGHTS_AT)
+        @pl.when(t == behind + PIECES - 1 + LAG_EXPERT + MID_EXPERT * middle)
         def _():
             for copies in own_of_core + mate_of_core:
                 for copy in copies:
@@ -176,31 +201,30 @@
     experts = router_t.shape[0]
     holder = lax.broadcasted_iota(jnp.int32, (experts, experts), 0)
     placed = (holder == placement[...]).astype(f32).astype(bf16)
-    expert_row = lax.broadcasted_iota(jnp.int32, (experts, rows), 0)
-    named = jnp.zeros((experts, rows), f32)
-    for k in range(routes_t.shape[0]):
-        named = named + (expert_row == routes_t[pl.ds(k, 1), :]).astype(f32)
-    named = jnp.dot(placed, named.astype(bf16), preferred_element_type=f32)
-    earlier = lax.broadcasted_iota(jnp.int32, (rows, rows), 0) < lax.broadcasted_iota(
-        jnp.int32, (rows, rows), 1
-    )
-    before = jnp.dot(named.astype(bf16), earlier.astype(f32).astype(bf16), preferred_element_type=f32)
-    slot = jnp.where(named > 0.5, before + 1.0, 0.0)
-    router_p = jnp.dot(placed, router_t[...], preferred_element_type=f32).astype(bf16)
-    logits = lax.dot_general(
-        router_p, normed, (((1,), (1,)), ((), ())), preferred_element_type=f32
-    )
-    picked = jnp.where(named > 0.5, jax.nn.sigmoid(logits), 0.0)
-    gates = picked / jnp.sum(picked, axis=0, keepdims=True)
-    for zz in range(NZ):
-        met[z, zz, pl.ds(0, NX), :] = slot[zz * NX : (zz + 1) * NX]
-        met[z, zz, pl.ds(NX, NX), :] = gates[zz * NX : (zz + 1) * NX]
+    router_p[...] = jnp.dot(placed, router_t[...], preferred_element_type=f32).astype(bf16)
+    named_by[z] = routes_t[...]
+
+    def tables(s):
+        expert_row = lax.broadcasted_iota(jnp.int32, (experts, rows), 0)
+        named = jnp.zeros((experts, rows), f32)
+        for k in range(routes_t.shape[0]):
+            named = named + (expert_row == named_by[s, pl.ds(k, 1), :]).astype(f32)
+        mapping = (lax.broadcasted_iota(jnp.int32, (experts, experts), 0) == placement[...]).astype(f32).astype(bf16)
+        named = jnp.dot(mapping, named.astype(bf16), preferred_element_type=f32)
+        earlier = lax.broadcasted_iota(jnp.int32, (rows, rows), 0) < lax.broadcasted_iota(
+            jnp.int32, (rows, rows), 1
+        )
+        before = jnp.dot(named.astype(bf16), earlier.astype(f32).astype(bf16), preferred_element_type=f32)
+        logits = lax.dot_general(
+            router_p[...], tok[s], (((1,), (1,)), ((), ())), preferred_element_type=f32
+        )
+        picked = jnp.where(named > 0.5, jax.nn.sigmoid(logits), 0.0)
+        met[s, pl.ds(0, experts), :] = jnp.where(named > 0.5, before + 1.0, 0.0)
+        met[s, pl.ds(experts, experts), :] = picked / jnp.sum(picked, axis=0, keepdims=True)
+
+    tables(z)
 
     piece = rows // PIECES
-    last = NZ - 1
-    behind_up = jnp.maximum(0, ((2 * z - last) * HOP + 3) // 4)
-    behind_down = jnp.maximum(0, ((last - 2 * z) * HOP + 3) // 4)
-
     def piece_at(p):
         return pl.ds(pl.multiple_of(p * piece, piece), piece)
 
@@ -209,7 +233,7 @@
         return remote(part_of, part_of, ag_s.at[way, s, p], ag_r.at[s, p], at_z(zz))
 
     def table_to(way, s, zz):
-        return remote(met.at[s], met.at[s], mg_s.at[way, s], mg_r.at[s], at_z(zz))
+        return remote(named_by.at[s], named_by.at[s], mg_s.at[way, s], mg_r.at[s], at_z(zz))
 
     def relay(way, k):
         t, p = k // PIECES, k % PIECES
@@ -236,53 +260,32 @@
         def _():
             piece_to(way, s, p, to).start()
 
-    def pair_at(tick, way):
-        k = tick - jnp.where(way == 0, behind_up, behind_down)
-        t = k // PIECES
-        whole = jnp.logical_and(jnp.logical_and(k >= 0, t < NZ), k % PIECES == PIECES - 1)
-        s = jnp.where(way == 0, t, last - t)
-        odd = t % 2 == 1
-        passed = jnp.logical_and(odd, jnp.where(way == 0, s < z, s > z))
-        own_t = jnp.maximum(1, jnp.where(way == 0, z - 1, last - 1 - z))
-        own = jnp.logical_and(z % 2 == 1 - way, t == own_t)
-        valid = jnp.logical_and(whole, jnp.logical_or(passed, own))
-        return jnp.where(valid, jnp.where(own, z // 2, s // 2), 0), valid
-
-    def spread(q, row):
-        pieces = []
-        token_block = lax.broadcasted_iota(jnp.int32, (1, 2 * rows), 1) // rows
-        for xx in range(NX):
-            both = jnp.concatenate(
-                [met[2 * q, z, pl.ds(row + xx, 1), :], met[2 * q + 1, z, pl.ds(row + xx, 1), :]], axis=1
-            )
-            for h in range(2):
-                pieces.append(jnp.where(token_block == h, both, 0.0))
-        return pieces
-
-    slot_of = lax.broadcasted_iota(jnp.int32, (CAP, 2 * rows), 0).astype(f32) + 1.0
-    pair_rows = 2 * CAP
+    slot_of = lax.broadcasted_iota(jnp.int32, (SLOTS, rows), 0).astype(f32) + 1.0
+    filled = pl.ds(0, CAP)
+
+    def lines(s, row):
+        return [met[s, pl.ds(row + z * NX + xx, 1), :] for xx in range(NX)]
 
     def gather(q):
-        pick = jnp.concatenate([(line == slot_of).astype(f32) for line in spread(q, 0)], axis=0).astype(bf16)
+        pick = jnp.concatenate([(line == slot_of).astype(f32) for line in lines(q, 0)], axis=0).astype(bf16)
 
         @pl.loop(0, width // 256)
         def _(n):
             cols = pl.ds(pl.multiple_of(n * 256, 256), 256)
-            pair = tok[pl.ds(2 * q, 2), :, cols].reshape(2 * rows, 256)
-            got = jnp.dot(pick, pair, preferred_element_type=f32).astype(bf16)
+            got = jnp.dot(pick, tok[q, :, cols], preferred_element_type=f32).astype(bf16)
             for xx in range(NX):
-                xs[q, xx, :, cols] = got[xx * pair_rows : (xx + 1) * pair_rows]
+                xs[q, xx, :, cols] = got[xx * SLOTS : (xx + 1) * SLOTS]
 
         for j in range(1, NX):
             to = (x + j) % NX
-            remote(xs.at[q, to], xr.at[q, x], xd_s.at[q, j], xd_r.at[q, j], at_x(to)).start()
-        xr[q, x] = xs[q, x]
+            remote(xs.at[q, to, filled], xr.at[q, x, filled], xd_s.at[q, j], xd_r.at[q, j], at_x(to)).start()
+        xr[q, x, filled] = xs[q, x, filled]
 
     def expert(q):
         for j in range(1, NX):
             src = (x + NX - j) % NX
-            remote(xs.at[q, src], xr.at[q, src], xd_s.at[q, j], xd_r.at[q, j], at_x(src)).wait_recv()
-        row_in = xr[q].reshape(NX * pair_rows, width)
+            remote(xs.at[q, src, filled], xr.at[q, src, filled], xd_s.at[q, j], xd_r.at[q, j], at_x(src)).wait_recv()
+        row_in = xr[q].reshape(NX * SLOTS, width)
 
         @pl.loop(0, ff // 256)
         def _(n):
@@ -299,21 +302,21 @@
             cols = pl.ds(pl.multiple_of(n * 256, 256), 256)
             got = jnp.dot(hidden, wdn[:, cols], preferred_element_type=f32).astype(bf16)
             for xx in range(NX):
-                ys[q, xx, :, cols] = got[xx * pair_rows : (xx + 1) * pair_rows]
+                ys[q, xx, :, cols] = got[xx * SLOTS : (xx + 1) * SLOTS]
 
         for j in range(1, NX):
             to = (x + j) % NX
-            remote(ys.at[q, to], yr.at[q, x], xb_s.at[q, j], xb_r.at[q, j], at_x(to)).start()
-        yr[q, x] = ys[q, x]
+            remote(ys.at[q, to, filled], yr.at[q, x, filled], xb_s.at[q, j], xb_r.at[q, j], at_x(to)).start()
+        yr[q, x, filled] = ys[q, x, filled]
 
     def mix(q):
         for j in range(1, NX):
             src = (x + NX - j) % NX
-            remote(ys.at[q, src], yr.at[q, src], xb_s.at[q, j], xb_r.at[q, j], at_x(src)).wait_recv()
+            remote(ys.at[q, src, filled], yr.at[q, src, filled], xb_s.at[q, j], xb_r.at[q, j], at_x(src)).wait_recv()
         weigh = jnp.concatenate(
             [
                 jnp.where(line == slot_of, gate, 0.0)
-                for line, gate in zip(spread(q, 0), spread(q, NX))
+                for line, gate in zip(lines(q, 0), lines(q, experts))
             ],
             axis=0,
         )
@@ -324,11 +327,11 @@
         @pl.loop(0, width // 256)
         def _(n):
             cols = pl.ds(pl.multiple_of(n * 256, 256), 256)
-            back = yr[q, :, :, cols].reshape(NX * pair_rows, 256)
+            back = yr[q, :, :, cols].reshape(NX * SLOTS, 256)
             total = jnp.dot(high, back, preferred_element_type=f32) + jnp.dot(
                 low, back, preferred_element_type=f32
             )
-            part[pl.ds(2 * q, 2), :, cols] = total.reshape(2, rows, 256)
+            part[q, :, cols] = total
 
     def add_and_send(way, k):
         r, p = k // PIECES, k % PIECES
@@ -354,28 +357,42 @@
 
             copy.start()
 
-    def stage(work, tick):
+    def stage(work, tick, up, down, with_own):
         def one(way, carry):
-            q, valid = pair_at(tick, way)
+            k = tick - jnp.where(way == 0, up, down)
+            s = jnp.where(way == 0, k // PIECES, last - k // PIECES)
+            comes = jnp.where(way == 0, s < z, s > z)
+            inside = jnp.logical_and(k >= 0, k < NZ * PIECES)
+            valid = jnp.logical_and(jnp.logical_and(inside, comes), k % PIECES == PIECES - 1)
+            valid = jnp.where(way == 2, k == PIECES - 1, valid)
+            s = jnp.where(way == 2, z, jnp.where(valid, s, 0))
 
             @pl.when(valid)
             def _():
-                work(q)
+                work(s)
 
             return carry
 
-        lax.fori_loop(0, 2, one, 0)
-
-    sum_down_at = behind_up + LAG_SUM + ((last - z) * 2 * HOP + 3) // 4
-    sum_up_at = behind_down + LAG_SUM + (z * 2 * HOP + 3) // 4
+        lax.fori_loop(0, 3 if with_own else 2, one, 0)
+
+    sum_down_at = behind_up + PIECES - 1 + LAG_MIX + ((last - z) * 2 * HOP + 3) // 4
+    sum_up_at = behind_down + PIECES - 1 + LAG_MIX + (z * 2 * HOP + 3) // 4
+
+    for s in range(NZ):
+        for xx in range(NX):
+            empty = jnp.zeros((SLOTS - CAP, width), bf16)
+            xr[s, xx, pl.ds(CAP, SLOTS - CAP)] = empty
+            yr[s, xx, pl.ds(CAP, SLOTS - CAP)] = empty
+    gather(z)
 
     def step(tick, carry):
-        weights_at(tick)
         relay(0, tick - behind_up)
         relay(1, tick - behind_down)
-        stage(gather, tick)
-        stage(expert, tick - LAG_EXPERT)
-        stage(mix, tick - LAG_MIX)
+        weights_at(tick)
+        stage(tables, tick, behind_up, behind_down, False)
+        stage(gather, tick, behind_up, behind_down, False)
+        stage(expert, tick - LAG_EXPERT - MID_EXPERT * middle, behind, behind, True)
+        stage(mix, tick - LAG_MIX - MID_MIX * middle, behind, behind, True)
         add_and_send(0, tick - sum_down_at)
         add_and_send(1, tick - sum_up_at)
         return carry
@@ -398,7 +415,8 @@
         out[at, :] = part[z, at].astype(bf16)
 
     for p in parts:
-        mate_out[p].wait_send()
+        for copy in mate_in[p]:
+            copy.wait_send()
         for j in range(NY):
             if j:
                 own_out[j][p].wait_send()
@@ -423,14 +441,14 @@
 
     lax.fori_loop(0, NZ, drain, 0)
 
-    def drain_pair(q, carry):
+    def drain_rows(q, carry):
         for j in range(1, NX):
             to = (x + j) % NX
-            remote(xs.at[q, to], xr.at[q, x], xd_s.at[q, j], xd_r.at[q, j], at_x(to)).wait_send()
-            remote(ys.at[q, to], yr.at[q, x], xb_s.at[q, j], xb_r.at[q, j], at_x(to)).wait_send()
+            remote(xs.at[q, to, filled], xr.at[q, x, filled], xd_s.at[q, j], xd_r.at[q, j], at_x(to)).wait_send()
+            remote(ys.at[q, to, filled], yr.at[q, x, filled], xb_s.at[q, j], xb_r.at[q, j], at_x(to)).wait_send()
         return carry
 
-    lax.fori_loop(0, NZ // 2, drain_pair, 0)
+    lax.fori_loop(0, NZ, drain_rows, 0)
 
     def drain_sum(s, carry):
         @pl.when(s != z)
@@ -459,7 +477,7 @@
     dma = pltpu.SemaphoreType.DMA
     vmem = pl.BlockSpec(memory_space=pltpu.VMEM)
     hbm = pl.BlockSpec(memory_space=pl.ANY)
-    rows_of = (NZ // 2, NX, 2 * CAP, width)
+    rows_of = (NZ, NX, SLOTS, width)
     return pl.pallas_call(
         kernel,
         out_shape=jax.ShapeDtypeStruct((rows, width), bf16),
@@ -467,25 +485,27 @@
         out_specs=vmem,
         scratch_shapes=[
             pltpu.VMEM((NZ, rows, width), bf16),
-            pltpu.VMEM((NZ, NZ, 2 * NX, rows), f32),
+            pltpu.VMEM((NZ, 2 * experts, rows), f32),
+            pltpu.VMEM((NZ, routes.shape[1], rows), jnp.int32),
+            pltpu.VMEM((experts, width), bf16),
             pltpu.VMEM((blks * grows, 2 * ff), bf16),
             pltpu.VMEM((blks * drows, width), bf16),
             pltpu.VMEM(rows_of, bf16),
             pltpu.VMEM(rows_of, bf16),
             pltpu.VMEM(rows_of, bf16),
             pltpu.VMEM(rows_of, bf16),
-            pltpu.VMEM((NX * 2 * CAP, ff), bf16),
+            pltpu.VMEM((NX * SLOTS, ff), bf16),
             pltpu.VMEM((NZ, rows, width), f32),
             pltpu.VMEM((NZ, rows, width), bf16),
             pltpu.VMEM((NZ, rows, width), bf16),
             pltpu.VMEM((NZ, rows, width), bf16),
             dma((3,)),
-            dma((3,)), dma((3,)),
+            dma((3, 3)), dma((3, 3)),
             dma((NY, 3)), dma((NY, 3)), dma((NY, 3)), dma((NY, 3)),
             dma((NY, 3)), dma((NY, 3)), dma((NY, 3)), dma((NY, 3)),
             dma((2, NZ, PIECES)), dma((NZ, PIECES)),
             dma((2, NZ)), dma((NZ,)),
-            dma((NZ // 2, NX)), dma((NZ // 2, NX)), dma((NZ // 2, NX)), dma((NZ // 2, NX)),
+            dma((NZ, NX)), dma((NZ, NX)), dma((NZ, NX)), dma((NZ, NX)),
             dma((NZ, PIECES)), dma((NZ, PIECES)), dma((NZ, PIECES)),
         ],
         compiler_params=pltpu.CompilerParams(

time: 205 us -> 191 us (0.932)
  the two profiles are of different devices: /device:TPU:134 before, /device:TPU:1 now
where the time goes in v3:
time: 191 us; the launch traced here: 189 us
  Pallas kernels  186 us (97%)
  local copies, waits for them, and re-layouts  3.05 us (2%)
    pallas_call x1, Pallas kernels, on_device(): pl.pallas_call(kernel, out_shape=jax.ShapeDtypeStruct((rows, width), bf16...  186 us

profile of v3, /device:TPU:1, one launch (start us, length us, event | category | flops | bytes accessed | tf_op | source)
XLA Modules:
  0.0 188.7 jit_solution(10837005007019521215)
XLA Ops:
  0.0 0.0 copy-start
  0.0 0.7 copy-done
  0.7 0.6 reshape.6.gain
  1.3 185.6 %shard_map.82 = bf16[128,1536]{1,0:T(8,128)(2,1)} custom-call(bf16[128,1536]{1,0:T(8,128)(2,1)} %tokens.1, bf16[1,1536]{1,0:T(2,128)(2,1)} %reshape.6.gain, s32[4,128]{1,0:T(4,128)} %bitcast.10, bf16[32,1536]{1,0:T(8,128)(2,1)} %bitcast.9, s32[1,32]{1,0:T(1,128)} %bitcast.11, bf16[96,768]{1,0:T(8,128)(2,1)} %bitcast.6, bf16[96,768]{1,0:T(8,128)(2,1)} %bitcast.7, ...), custom_call_target="tpu_custom_call" | custom-call | tf_op jit(solution)/shard_map/pallas_call | solution.py:481
  186.9 1.8 copy.10
Async XLA Ops:
  0.0 0.7 copy-start

commit v4 on v3

--- a/solution.py
+++ b/solution.py
@@ -11,8 +11,8 @@
 NZ, NX, NY = 8, 4, 4
 CAP = 24
 PIECES = 4
-LAG_EXPERT = 5
-LAG_MIX = 10
+LAG_EXPERT = 4
+LAG_MIX = 8
 MID_EXPERT = 2
 MID_MIX = 3
 HOP = 12

time: 191 us -> 189 us (0.990)
  Pallas kernels: 186 us -> 183 us
    pallas_call x1, Pallas kernels: 186 us -> 183 us  [on_device(): pl.pallas_call(kernel, out_shape=jax.ShapeDtypeStruct((rows, width), bf16...]
where the time goes in v4:
time: 189 us; the launch traced here: 186 us
  Pallas kernels  183 us (97%)
  local copies, waits for them, and re-layouts  3.05 us (2%)
    pallas_call x1, Pallas kernels, on_device(): pl.pallas_call(kernel, out_shape=jax.ShapeDtypeStruct((rows, width), bf16...  183 us

profile of v4, /device:TPU:1, one launch (start us, length us, event | category | flops | bytes accessed | tf_op | source)
XLA Modules:
  0.0 186.0 jit_solution(14702856584425555109)
XLA Ops:
  0.0 0.0 copy-start
  0.0 0.7 copy-done
  0.7 0.6 reshape.6.gain
  1.3 182.9 %shard_map.82 = bf16[128,1536]{1,0:T(8,128)(2,1)} custom-call(bf16[128,1536]{1,0:T(8,128)(2,1)} %tokens.1, bf16[1,1536]{1,0:T(2,128)(2,1)} %reshape.6.gain, s32[4,128]{1,0:T(4,128)} %bitcast.10, bf16[32,1536]{1,0:T(8,128)(2,1)} %bitcast.9, s32[1,32]{1,0:T(1,128)} %bitcast.11, bf16[96,768]{1,0:T(8,128)(2,1)} %bitcast.6, bf16[96,768]{1,0:T(8,128)(2,1)} %bitcast.7, ...), custom_call_target="tpu_custom_call" | custom-call | tf_op jit(solution)/shard_map/pallas_call | solution.py:481
  184.2 1.8 copy.10
Async XLA Ops:
  0.0 0.7 copy-start

commit v5 on v4

--- a/solution.py
+++ b/solution.py
@@ -18,10 +18,10 @@
 HOP = 12
 SLOTS = 32
 TICKS = (NZ - 1) * PIECES + ((NZ - 1) * HOP + 3) // 4 + PIECES + LAG_MIX + 4
-MATE_AT = (4, 6, 9)
+MATE_AT = (4, 7, 11)
 MATE_START = (-1, -1, -1, -1, 0, 1, 2, 3, 4)
 OWN_ROWS_AT = 5
-MATE_ROWS_AT = (8, 10, 12)
+MATE_ROWS_AT = (9, 12, 14)
 
 
 def kernel(

time: 189 us -> 191 us (1.011)
  the two profiles are of different devices: /device:TPU:1 before, /device:TPU:34 now
where the time goes in v5:
time: 191 us
  Pallas kernels  187 us (98%)
  local copies, waits for them, and re-layouts  3.05 us (2%)
    pallas_call x1, Pallas kernels, on_device(): pl.pallas_call(kernel, out_shape=jax.ShapeDtypeStruct((rows, width), bf16...  187 us

profile of v5, /device:TPU:34, one launch (start us, length us, event | category | flops | bytes accessed | tf_op | source)
XLA Modules:
  0.0 190.5 jit_solution(5358776868198551941)
XLA Ops:
  0.0 0.0 copy-start
  0.0 0.7 copy-done
  0.7 0.6 reshape.6.gain
  1.3 187.5 %shard_map.82 = bf16[128,1536]{1,0:T(8,128)(2,1)} custom-call(bf16[128,1536]{1,0:T(8,128)(2,1)} %tokens.1, bf16[1,1536]{1,0:T(2,128)(2,1)} %reshape.6.gain, s32[4,128]{1,0:T(4,128)} %bitcast.10, bf16[32,1536]{1,0:T(8,128)(2,1)} %bitcast.9, s32[1,32]{1,0:T(1,128)} %bitcast.11, bf16[96,768]{1,0:T(8,128)(2,1)} %bitcast.6, bf16[96,768]{1,0:T(8,128)(2,1)} %bitcast.7, ...), custom_call_target="tpu_custom_call" | custom-call | tf_op jit(solution)/shard_map/pallas_call | solution.py:481
  188.8 1.8 copy.10
Async XLA Ops:
  0.0 0.7 copy-start
